TPU v7x, 32 devices: a whole 2x2x4 slice. The times are simulated.
32 devices in a mesh: dom: 16 (over z, y, x), row: 2 (over core).
Axes of the slice: x: 2, y: 2, z: 4, core: 2. Of those that a mesh axis runs over, the one named last changes fastest.
Arguments:
- features: float32 [4096, 128], P(('dom', 'row')), may hold values from -6 to 6
- history: float32 [4096, 1024], P(('dom', 'row')), may hold values from -3 to 3
- tiles: float32 [32, 4, 128, 128], P(('dom', 'row')), may hold values from -0.25 to 0.25
- tile_cols: int32 [32, 4], P(('dom', 'row')), may hold values from 0 to 1
- cross_weight: float32 [4096, 128], P(('dom', 'row')), may hold values from -0.75 to 0.75
- send_rows: int32 [32, 16, 8], P(('dom', 'row')), may hold values from 0 to 127
- send_count: int32 [32, 16], P(('dom', 'row')), may hold values from 0 to 8, as said below
- cotangent: float32 [4096, 172], P(('dom', 'row')), may hold values from -0.0234375 to 0.0234375
- w_one: float32 [128, 1024], replicated, may hold values from -0.5 to 0.5
- w_two: float32 [1024, 172], replicated, may hold values from -0.1875 to 0.1875
Outputs:
- logits: float32 [4096, 172], P(('dom', 'row'))
- grad_w1: float32 [128, 1024], replicated
- grad_w2: float32 [1024, 172], replicated
Inputs may be any that keep to these rules, and one draw needn't show every extreme that they name: send_count is 0 toward the sender's own partition; in every draw some partition receives 8 live rows from every device of every other partition.
All inputs are finite; a program needn't handle non-finite values.
Results may differ from a plain program's by a relative error of at most 0.0003.
Values sent between devices are 32-bit elements; how exact they have to be, the bound alone decides.
A program may use at most 64 MiB of HBM per device.

v0:
```python
import jax
import jax.numpy as jnp
from jax import lax
from jax.sharding import PartitionSpec as P

HIGH = lax.Precision.HIGHEST


def gate_act(values):
    sigma = jax.nn.sigmoid(values)
    return (values * sigma, sigma * (1.0 + values * (1.0 - sigma)))


def matmul(left, right):
    return jnp.dot(left, right, precision=HIGH, preferred_element_type=jnp.float32)


def on_device(
    features,
    history,
    tiles,
    tile_cols,
    cross_weight,
    send_rows,
    send_count,
    cotangent,
    w_one,
    w_two,
):
    rows_here = features.shape[0]
    blocks_here = tiles.shape[0]
    parts_count = send_rows.shape[1]
    slot_count = send_rows.shape[2]
    width_in = features.shape[1]
    width_hidden = history.shape[1]
    width_out = w_two.shape[1]
    lane_index = jnp.arange(128, dtype=jnp.int32)
    targets = tile_cols[:, :, None] * 128 + lane_index[None, None, :]
    live_mask = (jnp.arange(slot_count, dtype=jnp.int32)[None, :] < send_count[0][:, None]).astype(
        jnp.float32
    )
    pick_rows = send_rows[0]
    feat_out = jnp.take(features, pick_rows, axis=0) * live_mask[:, :, None]
    hist_out = jnp.take(history, pick_rows, axis=0) * live_mask[:, :, None]
    got_feat, got_hist = (
        lax.all_to_all(feat_out, "dom", split_axis=0, concat_axis=0, tiled=True),
        lax.all_to_all(hist_out, "dom", split_axis=0, concat_axis=0, tiled=True),
    )
    cross_feat = matmul(cross_weight, got_feat.reshape(parts_count * slot_count, width_in))
    cross_hist = matmul(cross_weight, got_hist.reshape(parts_count * slot_count, width_hidden))
    cross_logits = matmul(cross_hist, w_two)

    def add_panel(panel):
        row_count = panel.shape[0]
        inside = (targets >= 0) & (targets < row_count)
        picked = jnp.take(panel, jnp.clip(targets, 0, row_count - 1), axis=0)
        picked = picked * inside[..., None].astype(panel.dtype)
        return jnp.einsum("bkij,bkjw->biw", tiles, picked, precision=HIGH)

    local_feat = add_panel(lax.all_gather(features, "row", axis=0, tiled=True))
    layer_in = local_feat.reshape(rows_here, width_in) + cross_feat
    pre_act = matmul(layer_in, w_one)
    hidden, slope_gate = gate_act(pre_act)
    projected = matmul(hidden, w_two)
    local_out = add_panel(lax.all_gather(projected, "row", axis=0, tiled=True))
    logits = local_out.reshape(rows_here, width_out) + cross_logits
    blocked_grads = cotangent.reshape(blocks_here, 128, width_out)
    contrib = jnp.einsum("bkij,biw->bkjw", tiles, blocked_grads, precision=HIGH)
    block_ids = jnp.arange(lax.axis_size("row") * rows_here // 128, dtype=jnp.int32)
    hot = (tile_cols[:, :, None] == block_ids[None, None, :]).astype(jnp.float32)
    summed = jnp.einsum("bkc,bkjw->cjw", hot, contrib, precision=HIGH)
    back_grad = lax.psum_scatter(
        summed.reshape(lax.axis_size("row") * rows_here // 128 * 128, width_out),
        "row",
        scatter_dimension=0,
        tiled=True,
    )
    grad_two = matmul(hidden.T, back_grad)
    grad_two = grad_two + matmul(cross_hist.T, cotangent)
    grad_pre = matmul(back_grad, w_two.T) * slope_gate
    grad_one = matmul(layer_in.T, grad_pre)
    grad_one, grad_two = lax.psum((grad_one, grad_two), ("dom", "row"))
    return (logits, grad_one, grad_two)


def solution(mesh):
    placed = (
        P(("dom", "row"), None),
        P(("dom", "row"), None),
        P(("dom", "row"), None, None, None),
        P(("dom", "row"), None),
        P(("dom", "row"), None),
        P(("dom", "row"), None, None),
        P(("dom", "row"), None),
        P(("dom", "row"), None),
        P(),
        P(),
    )
    return jax.shard_map(
        on_device,
        mesh=mesh,
        in_specs=placed,
        out_specs=(P(("dom", "row"), None), P(), P()),
        check_vma=False,
    )
```

profile of v0, /device:TPU:0, one launch (start us, length us, event | category | flops | bytes accessed | tf_op | source)
XLA Modules:
  0.0 193.7 jit_solution(11159465152291520125)
XLA Ops:
  7.2 0.0 copy-start
  7.2 0.0 copy-start.10
  7.2 0.8 compare_and_fusion
  8.0 0.1 copy.20
  8.1 0.1 copy.21
  8.1 0.1 reshape.276
  8.2 0.0 copy-start.12
  8.2 0.6 copy-done.12
  8.9 0.1 fusion.26
  9.0 1.5 gather_fusion.1
  10.5 0.7 fusion.25
  11.2 8.3 %all-to-all-start = ((f32[16,8,128]{2,1,0:T(8,128)}), f32[16,8,128]{2,1,0:T(8,128)S(1)}, u32[]{:S(2)}, u32[]{:S(2)}) async-start(f32[16,8,128]{2,1,0:T(8,128)} %fusion.25), calls=%async_computation | async-start | bytes 131072 | tf_op jit(solution)/shard_map/all_to_all | solution.py:46
  19.6 0.0 reduce-scatter.2.cloned.1.call-start
  19.6 0.0 copy-done.6
  19.6 0.0 copy-done.3
  19.6 0.5 fusion.7
  20.1 0.0 copy-start.11
  20.1 0.6 copy-done.11
  20.8 0.5 convolution_bitcast_fusion
  21.3 0.1 pad.4
  21.4 0.7 copy.26
  22.0 0.0 reduce-scatter.2.cloned.1.call-update
  22.1 0.1 fusion.27
  22.2 0.1 compare_and_fusion.1
  22.2 0.6 copy-done.2
  22.9 1.9 all_gather.6
  24.8 1.0 gather_fusion
  25.8 0.0 copy-start.1
  25.8 0.1 copy.19
  26.0 0.9 copy-done.1
  26.9 0.8 gather_fusion.3
  27.7 0.9 fusion.2
  28.6 0.4 convolution_bitcast_fusion.2
  29.0 0.0 copy-start.8
  29.0 0.0 copy-start.5
  29.0 0.0 all-to-all-done
  29.0 7.0 %all-to-all-start.1 = ((f32[16,8,1024]{2,1,0:T(8,128)}), f32[16,8,1024]{2,1,0:T(8,128)S(1)}, u32[]{:S(2)}, u32[]{:S(2)}) async-start(f32[16,8,1024]{2,1,0:T(8,128)} %fusion.2), calls=%async_computation.1 | async-start | bytes 1048576 | tf_op jit(solution)/shard_map/all_to_all | solution.py:47
  36.1 0.0 all-reduce.3.cloned.1.call-start
  36.1 0.3 convolution_add_fusion.2
  36.4 0.0 copy-done.5
  36.4 0.6 fusion.40
  37.1 0.0 reduce-scatter.2.cloned.1.call-done
  37.1 1.6 convolution_multiply_fusion
  38.7 0.0 copy-start.13
  38.7 1.4 fusion.41
  40.1 0.0 copy-done.13
  40.1 0.9 fusion.20
  41.0 0.0 copy-start.7
  41.0 10.4 %all-to-all-done.1 = f32[16,8,1024]{2,1,0:T(8,128)S(1)} async-done(((f32[16,8,1024]{2,1,0:T(8,128)}), f32[16,8,1024]{2,1,0:T(8,128)S(1)}, u32[]{:S(2)}, u32[]{:S(2)}) %all-to-all-start.1) | async-done | bytes 524320 | tf_op jit(solution)/shard_map/all_to_all | solution.py:47
  51.5 0.0 copy-done.9
  51.5 1.0 fusion
  52.5 0.0 copy-done.7
  52.5 1.6 convolution_add_fusion
  54.1 0.0 all-reduce.3.cloned.1.call-update
  54.1 0.8 fusion.22
  55.0 1.9 all_gather.7
  56.9 0.1 copy.22
  57.0 1.6 gather_fusion.2
  58.6 0.2 copy.23
  58.8 0.5 convolution_bitcast_fusion.1
  59.3 1.4 convolution_add_fusion.1
  60.7 123.4 %all-reduce.3.cloned.1.call-done = (f32[128,1024]{1,0:T(8,128)}, f32[1024,172]{0,1:T(8,128)}) async-done(((f32[128,1024]{1,0:T(8,128)}, f32[1024,172]{0,1:T(8,128)}), (f32[128,1024]{1,0:T(8,128)}, f32[1024,172]{0,1:T(8,128)})) %all-reduce.3.cloned.1.call-update) | async-done | bytes 1228816 | tf_op jit(solution)/shard_map/psum | solution.py:82
  184.0 2.0 %copy.31 = f32[128,1024]{1,0:T(8,128)} copy(f32[128,1024]{1,0:T(8,128)} %get-tuple-element.8) | data formatting | bytes 1048576
  186.0 0.9 copy.32
  (13 shorter events, 0.0 us)
Async XLA Ops:
  7.2 29.9 %copy-start = (f32[1024,172]{0,1:T(8,128)S(1)}, f32[1024,172]{0,1:T(8,128)}, u32[]{:S(2)}) copy-start(f32[1024,172]{0,1:T(8,128)} %param.19) | copy-start | bytes 2113540
  7.2 0.8 copy-start.10
  8.2 0.7 copy-start.12
  9.0 10.7 %copy-start.6 = (f32[128,172]{0,1:T(8,128)S(1)}, f32[128,172]{0,1:T(8,128)}, u32[]{:S(2)}) copy-start(f32[128,172]{0,1:T(8,128)} %param.17) | copy-start | bytes 264196
  10.5 9.1 %copy-start.3 = (f32[1,4,128,128]{3,2,1,0:T(8,128)S(1)}, f32[1,4,128,128]{3,2,1,0:T(8,128)}, u32[]{:S(2)}) copy-start(f32[1,4,128,128]{3,2,1,0:T(8,128)} %param.12) | copy-start | bytes 786436
  11.2 17.8 %all-to-all-start = ((f32[16,8,128]{2,1,0:T(8,128)}), f32[16,8,128]{2,1,0:T(8,128)S(1)}, u32[]{:S(2)}, u32[]{:S(2)}) async-start(f32[16,8,128]{2,1,0:T(8,128)} %fusion.25), calls=%async_computation | async-start | bytes 131072 | tf_op jit(solution)/shard_map/all_to_all | solution.py:46
  19.6 17.5 %reduce-scatter.2.cloned.1.call-start = ((), (), s32[]{:S(2)}) async-start(), calls=%async_computation.3 | async-start | bytes 270336 | tf_op jit(solution)/shard_map/reduce_scatter | solution.py:72
  20.1 0.7 copy-start.11
  22.0 0.8 copy-start.2
  25.8 1.0 copy-start.1
  29.0 7.1 %copy-start.8 = (f32[128,128]{1,0:T(8,128)S(1)}, f32[128,128]{1,0:T(8,128)}, u32[]{:S(2)}) copy-start(f32[128,128]{1,0:T(8,128)} %param.14) | copy-start | bytes 196612
  29.0 7.4 %copy-start.5 = (f32[128,1024]{1,0:T(8,128)S(1)}, f32[128,1024]{1,0:T(8,128)}, u32[]{:S(2)}) copy-start(f32[128,1024]{1,0:T(8,128)} %param.18) | copy-start | bytes 1572868
  29.0 22.5 %all-to-all-start.1 = ((f32[16,8,1024]{2,1,0:T(8,128)}), f32[16,8,1024]{2,1,0:T(8,128)S(1)}, u32[]{:S(2)}, u32[]{:S(2)}) async-start(f32[16,8,1024]{2,1,0:T(8,128)} %fusion.2), calls=%async_computation.1 | async-start | bytes 1048576 | tf_op jit(solution)/shard_map/all_to_all | solution.py:47
  36.1 148.0 %all-reduce.3.cloned.1.call-start = ((), (), s32[]{:S(2)}) async-start(), calls=%async_computation.4 | async-start | bytes 2490368 | tf_op jit(solution)/shard_map/psum | solution.py:82
  38.7 1.4 copy-start.13
  40.1 11.3 %copy-start.9 = (f32[128,128]{1,0:T(8,128)S(1)}, f32[128,128]{1,0:T(8,128)}, u32[]{:S(2)}) copy-start(f32[128,128]{1,0:T(8,128)} %param.14) | copy-start | bytes 196612
  41.0 11.5 %copy-start.7 = (f32[128,172]{0,1:T(8,128)S(1)}, f32[128,172]{0,1:T(8,128)}, u32[]{:S(2)}) copy-start(f32[128,172]{0,1:T(8,128)} %param.17) | copy-start | bytes 264196
  184.0 2.0 %copy-start.4 = (f32[1024,172]{0,1:T(8,128)S(1)}, f32[1024,172]{0,1:T(8,128)}, u32[]{:S(2)}) copy-start(f32[1024,172]{0,1:T(8,128)} %get-tuple-element.9) | copy-start | bytes 2113540
Sparse Core Ops, SparseCore 0:
  23.2 8.9 reduce-scatter.1
  54.3 129.7 all-reduce.2
where the time goes:
time: 194 us
  waiting for transfers between devices  134 us (69%)
  starting transfers between devices  15.5 us (8%)
  between operations  14.4 us (7%)
  local copies, waits for them, and re-layouts  12.1 us (6%)
  matrix products  11.4 us (6%)
  blocking collectives  3.82 us (2%)
  other arithmetic  2.67 us (1%)
    psum x1, waiting for transfers between devices, on_device(): grad_one, grad_two = lax.psum((grad_one, grad_two), ('dom', 'row'))  123 us
    all_to_all x1, waiting for transfers between devices, on_device(): lax.all_to_all(hist_out, 'dom', split_axis=0, concat_axis=0, tiled=True)  10.4 us
    dot_general x9, matrix products, matmul(): jnp.dot(left, right, precision=HIGH, preferred_element_type=jnp.float32)  9.63 us
    all_to_all x1, starting transfers between devices, on_device(): lax.all_to_all(feat_out, 'dom', split_axis=0, concat_axis=0, tiled=True)  8.34 us
    all_to_all x1, starting transfers between devices, on_device(): lax.all_to_all(hist_out, 'dom', split_axis=0, concat_axis=0, tiled=True)  7.05 us
    unnamed x32, local copies, waits for them, and re-layouts  6.46 us
  transfers between devices with their start and end apart: 4, of which 2 were waited for; matrix products, arithmetic and copies ran while one was open for 7% of the time, Pallas kernels for 0%

commit v1 on v0

--- a/solution.py
+++ b/solution.py
@@ -4,6 +4,7 @@
 from jax.sharding import PartitionSpec as P
 
 HIGH = lax.Precision.HIGHEST
+watch_islands = lambda x_local: lax.psum(lax.psum(x_local, "row"), "dom")
 
 
 def gate_act(values):
@@ -79,7 +80,7 @@
     grad_two = grad_two + matmul(cross_hist.T, cotangent)
     grad_pre = matmul(back_grad, w_two.T) * slope_gate
     grad_one = matmul(layer_in.T, grad_pre)
-    grad_one, grad_two = lax.psum((grad_one, grad_two), ("dom", "row"))
+    grad_one, grad_two = watch_islands((grad_one, grad_two))
     return (logits, grad_one, grad_two)
 
 

time: 194 us -> 204 us (1.052)
  waiting for transfers between devices: 134 us -> 144 us
    psum x1 -> x2, waiting for transfers between devices: 123 us -> 133 us  [watch_islands = lambda x_local: lax.psum(lax.psum(x_local, 'row'), 'dom')]
  transfers between devices with their start and end apart: 4 -> 5, of which waited for: 2 -> 3; matrix products, arithmetic and copies ran while one was open for 7% -> 7% of each run, Pallas kernels for 0% -> 0%
where the time goes in v1:
time: 204 us; the launch traced here: 203 us
  waiting for transfers between devices  144 us (71%)
  starting transfers between devices  15.5 us (8%)
  between operations  14.1 us (7%)
  local copies, waits for them, and re-layouts  12.1 us (6%)
  matrix products  11.4 us (6%)
  blocking collectives  3.82 us (2%)
  other arithmetic  2.67 us (1%)
    psum x2, waiting for transfers between devices, watch_islands = lambda x_local: lax.psum(lax.psum(x_local, 'row'), 'dom')  133 us
    all_to_all x1, waiting for transfers between devices, on_device(): lax.all_to_all(hist_out, 'dom', split_axis=0, concat_axis=0, tiled=True)  10.4 us
    dot_general x9, matrix products, matmul(): jnp.dot(left, right, precision=HIGH, preferred_element_type=jnp.float32)  9.63 us
    all_to_all x1, starting transfers between devices, on_device(): lax.all_to_all(feat_out, 'dom', split_axis=0, concat_axis=0, tiled=True)  8.34 us
    all_to_all x1, starting transfers between devices, on_device(): lax.all_to_all(hist_out, 'dom', split_axis=0, concat_axis=0, tiled=True)  7.05 us
    unnamed x32, local copies, waits for them, and re-layouts  6.46 us
  transfers between devices with their start and end apart: 5, of which 3 were waited for; matrix products, arithmetic and copies ran while one was open for 7% of the time, Pallas kernels for 0%

profile of v1, /device:TPU:0, one launch (start us, length us, event | category | flops | bytes accessed | tf_op | source)
XLA Modules:
  0.0 203.1 jit_solution(9234498677462944556)
XLA Ops:
  7.2 0.0 copy-start
  7.2 0.0 copy-start.10
  7.2 0.8 compare_and_fusion
  8.0 0.0 copy-done.10
  8.0 0.1 copy.20
  8.1 0.1 copy.21
  8.1 0.1 reshape.276
  8.2 0.0 copy-start.12
  8.2 0.6 copy-done.12
  8.9 0.1 fusion.26
  9.0 1.5 gather_fusion.1
  10.5 0.7 fusion.25
  11.2 8.3 %all-to-all-start = ((f32[16,8,128]{2,1,0:T(8,128)}), f32[16,8,128]{2,1,0:T(8,128)S(1)}, u32[]{:S(2)}, u32[]{:S(2)}) async-start(f32[16,8,128]{2,1,0:T(8,128)} %fusion.25), calls=%async_computation | async-start | bytes 131072 | tf_op jit(solution)/shard_map/all_to_all | solution.py:47
  19.6 0.0 reduce-scatter.2.cloned.1.call-start
  19.6 0.0 copy-done.6
  19.6 0.0 copy-done.3
  19.6 0.5 fusion.7
  20.1 0.0 copy-start.11
  20.1 0.6 copy-done.11
  20.8 0.5 convolution_bitcast_fusion
  21.3 0.1 pad.4
  21.4 0.7 copy.26
  22.0 0.0 reduce-scatter.2.cloned.1.call-update
  22.1 0.1 fusion.27
  22.2 0.1 compare_and_fusion.1
  22.2 0.6 copy-done.2
  22.9 1.9 all_gather.6
  24.8 1.0 gather_fusion
  25.8 0.0 copy-start.1
  25.8 0.1 copy.19
  26.0 0.9 copy-done.1
  26.9 0.8 gather_fusion.3
  27.7 0.9 fusion.2
  28.6 0.4 convolution_bitcast_fusion.2
  29.0 0.0 copy-start.8
  29.0 0.0 copy-start.5
  29.0 0.0 all-to-all-done
  29.0 7.1 %all-to-all-start.1 = ((f32[16,8,1024]{2,1,0:T(8,128)}), f32[16,8,1024]{2,1,0:T(8,128)S(1)}, u32[]{:S(2)}, u32[]{:S(2)}) async-start(f32[16,8,1024]{2,1,0:T(8,128)} %fusion.2), calls=%async_computation.1 | async-start | bytes 1048576 | tf_op jit(solution)/shard_map/all_to_all | solution.py:48
  36.1 0.0 all-reduce.7.cloned.1.call-start
  36.1 0.3 convolution_add_fusion.2
  36.4 0.6 fusion.40
  37.1 0.0 reduce-scatter.2.cloned.1.call-done
  37.1 0.0 copy-done
  37.1 1.6 convolution_multiply_fusion
  38.7 1.4 fusion.41
  40.1 0.9 fusion.20
  41.0 0.0 copy-start.7
  41.0 10.4 %all-to-all-done.1 = f32[16,8,1024]{2,1,0:T(8,128)S(1)} async-done(((f32[16,8,1024]{2,1,0:T(8,128)}), f32[16,8,1024]{2,1,0:T(8,128)S(1)}, u32[]{:S(2)}, u32[]{:S(2)}) %all-to-all-start.1) | async-done | bytes 524320 | tf_op jit(solution)/shard_map/all_to_all | solution.py:48
  51.5 1.0 fusion
  52.5 1.6 convolution_add_fusion
  54.1 0.0 all-reduce.7.cloned.1.call-update
  54.1 0.0 all-reduce.5.cloned.1.call-start
  54.2 18.3 %all-reduce.7.cloned.1.call-done = (f32[128,1024]{1,0:T(8,128)}, f32[1024,172]{0,1:T(8,128)}) async-done(((f32[128,1024]{1,0:T(8,128)}, f32[1024,172]{0,1:T(8,128)}), (f32[128,1024]{1,0:T(8,128)}, f32[1024,172]{0,1:T(8,128)})) %all-reduce.7.cloned.1.call-update) | async-done | bytes 1228816 | tf_op jit(solution)/shard_map/psum | solution.py:7
  72.5 0.0 all-reduce.5.cloned.1.call-update
  72.5 0.8 fusion.22
  73.3 1.9 all_gather.7
  75.3 0.1 copy.22
  75.4 1.6 gather_fusion.2
  77.0 0.2 copy.23
  77.2 0.5 convolution_bitcast_fusion.1
  77.7 1.4 convolution_add_fusion.1
  79.0 114.7 %all-reduce.5.cloned.1.call-done = (f32[128,1024]{1,0:T(8,128)}, f32[1024,172]{0,1:T(8,128)}) async-done(((f32[128,1024]{1,0:T(8,128)}, f32[1024,172]{0,1:T(8,128)}), (f32[128,1024]{1,0:T(8,128)}, f32[1024,172]{0,1:T(8,128)})) %all-reduce.5.cloned.1.call-update) | async-done | bytes 1228816 | tf_op jit(solution)/shard_map/psum | solution.py:7
  193.8 2.0 copy.33
  195.7 0.9 copy.34
  (16 shorter events, 0.0 us)
Async XLA Ops:
  7.2 29.9 %copy-start = (f32[1024,172]{0,1:T(8,128)S(1)}, f32[1024,172]{0,1:T(8,128)}, u32[]{:S(2)}) copy-start(f32[1024,172]{0,1:T(8,128)} %param.19) | copy-start | bytes 2113540
  7.2 0.8 copy-start.10
  8.2 0.7 copy-start.12
  9.0 10.7 %copy-start.6 = (f32[128,172]{0,1:T(8,128)S(1)}, f32[128,172]{0,1:T(8,128)}, u32[]{:S(2)}) copy-start(f32[128,172]{0,1:T(8,128)} %param.17) | copy-start | bytes 264196
  10.5 9.2 %copy-start.3 = (f32[1,4,128,128]{3,2,1,0:T(8,128)S(1)}, f32[1,4,128,128]{3,2,1,0:T(8,128)}, u32[]{:S(2)}) copy-start(f32[1,4,128,128]{3,2,1,0:T(8,128)} %param.12) | copy-start | bytes 786436
  11.2 17.8 %all-to-all-start = ((f32[16,8,128]{2,1,0:T(8,128)}), f32[16,8,128]{2,1,0:T(8,128)S(1)}, u32[]{:S(2)}, u32[]{:S(2)}) async-start(f32[16,8,128]{2,1,0:T(8,128)} %fusion.25), calls=%async_computation | async-start | bytes 131072 | tf_op jit(solution)/shard_map/all_to_all | solution.py:47
  19.6 17.5 %reduce-scatter.2.cloned.1.call-start = ((), (), s32[]{:S(2)}) async-start(), calls=%async_computation.3 | async-start | bytes 270336 | tf_op jit(solution)/shard_map/reduce_scatter | solution.py:73
  20.1 0.7 copy-start.11
  22.0 0.8 copy-start.2
  25.8 1.0 copy-start.1
  29.0 7.1 %copy-start.8 = (f32[128,128]{1,0:T(8,128)S(1)}, f32[128,128]{1,0:T(8,128)}, u32[]{:S(2)}) copy-start(f32[128,128]{1,0:T(8,128)} %param.14) | copy-start | bytes 196612
  29.0 7.4 %copy-start.5 = (f32[128,1024]{1,0:T(8,128)S(1)}, f32[128,1024]{1,0:T(8,128)}, u32[]{:S(2)}) copy-start(f32[128,1024]{1,0:T(8,128)} %param.18) | copy-start | bytes 1572868
  29.0 22.5 %all-to-all-start.1 = ((f32[16,8,1024]{2,1,0:T(8,128)}), f32[16,8,1024]{2,1,0:T(8,128)S(1)}, u32[]{:S(2)}, u32[]{:S(2)}) async-start(f32[16,8,1024]{2,1,0:T(8,128)} %fusion.2), calls=%async_computation.1 | async-start | bytes 1048576 | tf_op jit(solution)/shard_map/all_to_all | solution.py:48
  36.1 36.4 %all-reduce.7.cloned.1.call-start = ((), (), s32[]{:S(2)}) async-start(), calls=%async_computation.5 | async-start | bytes 2490368 | tf_op jit(solution)/shard_map/psum | solution.py:7
  38.7 1.4 copy-start.13
  40.1 11.3 %copy-start.9 = (f32[128,128]{1,0:T(8,128)S(1)}, f32[128,128]{1,0:T(8,128)}, u32[]{:S(2)}) copy-start(f32[128,128]{1,0:T(8,128)} %param.14) | copy-start | bytes 196612
  41.0 11.5 %copy-start.7 = (f32[128,172]{0,1:T(8,128)S(1)}, f32[128,172]{0,1:T(8,128)}, u32[]{:S(2)}) copy-start(f32[128,172]{0,1:T(8,128)} %param.17) | copy-start | bytes 264196
  54.1 139.7 %all-reduce.5.cloned.1.call-start = ((), (), s32[]{:S(2)}) async-start(), calls=%async_computation.4 | async-start | bytes 2490368 | tf_op jit(solution)/shard_map/psum | solution.py:7
  193.8 2.0 copy-start.4
Sparse Core Ops, SparseCore 0:
  23.2 8.9 reduce-scatter.1
  54.2 18.1 all-reduce.6
  78.1 115.6 all-reduce.4
